TPU v7x, 256 devices: a whole 4x4x8 slice. The times are simulated.
256 devices in a mesh: segment: 4 (over x), gz: 64 (over y, z, core).
Axes of the slice: x: 4, y: 4, z: 8, core: 2. Of those that a mesh axis runs over, the one named last changes fastest.
Arguments:
- start_volume: float32 [4, 1024, 1024], P(None, 'gz'), may hold values from -6 to 6
- sinogram: float32 [4, 1024, 1024], P(None, 'gz'), may hold values from -6 to 6
- offsets: int32 [4, 8], replicated, may hold values from -15 to 15, as said below
- projector: bfloat16 [3, 1024, 1024], replicated, may hold values from -0.109375 to 0.109375
- dual_in: bfloat16 [32, 27], replicated, may hold values from -1.25 to 1.25
- dual_out: bfloat16 [9, 32], replicated, may hold values from -0.375 to 0.375
- primal_in: bfloat16 [64, 54], replicated, may hold values from -0.875 to 0.875
- primal_out: bfloat16 [27, 64], replicated, may hold values from -0.15625 to 0.15625
Outputs:
- volume: float32 [4, 1024, 1024], P('segment', 'gz')
Inputs may be any that keep to these rules, and one draw needn't show every extreme that they name: `offsets`: both ends of the range are taken in every draw.
All inputs are finite; a program needn't handle non-finite values.
Results may differ from a plain program's by a relative error of at most 0.005.
Values may be sent and summed in bfloat16 or wider, within the bound.
A program may use at most 64 MiB of HBM per device.

v0:
```python
import jax
import jax.numpy as jnp
from jax import lax
from jax.sharding import PartitionSpec as P

IMG = 32
NCOL = 128
ITERS = 2


def padded_2(cells, sides, width):
    for axis, dim in sides:
        count = lax.axis_size(axis)
        ends = count - 1
        head = lax.slice_in_dim(cells, 0, width, axis=dim)
        tail = lax.slice_in_dim(cells, cells.shape[dim] - width, cells.shape[dim], axis=dim)
        cells = jnp.concatenate(
            [
                lax.ppermute(tail, axis, [(i, (i + 1) % count) for i in range(ends)]),
                cells,
                lax.ppermute(head, axis, [((i + 1) % count, i) for i in range(ends)]),
            ],
            axis=dim,
        )
    return cells


def as_sent(x):
    return jax.tree.map(lambda a: a.astype(jnp.bfloat16) if a.dtype == jnp.float32 else a, x)


def shifted_2(value, axis, steps):
    count = lax.axis_size(axis)
    pairs = [(source, (source + steps) % count) for source in range(count)]
    return lax.ppermute(value, axis, pairs)


def plane_taps(flavour):
    cell_count = IMG * IMG
    positions = jnp.arange(cell_count, dtype=jnp.int32)
    tap_list = []
    if flavour == 0:
        column_of = positions % NCOL
        for step_size in (-1, 0, 1):
            keep_mask = ((column_of + step_size >= 0) & (column_of + step_size < NCOL)).astype(
                jnp.float32
            )
            tap_list.append((step_size, keep_mask))
    else:
        row_of = positions // IMG
        column_of = positions % IMG
        for down_step in (-1, 0, 1):
            for across_step in (-1, 0, 1):
                keep_mask = (
                    (row_of + down_step >= 0)
                    & (row_of + down_step < IMG)
                    & (column_of + across_step >= 0)
                    & (column_of + across_step < IMG)
                ).astype(jnp.float32)
                tap_list.append((down_step * IMG + across_step, keep_mask))
    return tap_list


def plane_shift(values, offset, keep_mask):
    margin = IMG + 1
    cell_count = values.shape[-1]
    widths = [(0, 0)] * (values.ndim - 1) + [(margin, margin)]
    padded = jnp.pad(values, widths)
    shifted = lax.slice_in_dim(
        padded, margin + offset, margin + offset + cell_count, axis=values.ndim - 1
    )
    return shifted * keep_mask.astype(values.dtype)


def expand(source, row_count, tap_list):
    pieces = []
    for depth_index in range(3):
        layer_rows = lax.slice_in_dim(source, depth_index, depth_index + row_count, axis=1)
        for offset, keep_mask in tap_list:
            pieces.append(plane_shift(layer_rows, offset, keep_mask))
    return jnp.concatenate(pieces, axis=0)


def collapse(hidden, w_out, row_count, tap_list):
    partial_value = jnp.einsum("to,ozn->tzn", w_out, hidden, preferred_element_type=jnp.float32)
    summed = jnp.zeros((row_count, hidden.shape[2]), jnp.float32)
    tap_number = 0
    for depth_index in range(3):
        for offset, keep_mask in tap_list:
            layer_rows = lax.slice_in_dim(
                partial_value[tap_number], depth_index, depth_index + row_count, axis=0
            )
            summed = summed + plane_shift(layer_rows, offset, keep_mask)
            tap_number = tap_number + 1
    return summed


def first_layer(extended, row_count, net_mode, weights):
    dual_in, dual_out, primal_in, primal_out = weights
    hidden_count = primal_in.shape[0]
    pad_count = hidden_count - dual_in.shape[0]
    cell_count = extended.shape[2]

    def first_dual_branch(source):
        columns = expand(source, row_count, plane_taps(0))
        hidden = jax.nn.relu(
            jnp.einsum("ok,kzn->ozn", dual_in, columns, preferred_element_type=jnp.float32)
        ).astype(jnp.bfloat16)
        return jnp.pad(hidden, ((0, pad_count), (0, 0), (0, 0)))

    def first_primal_branch(source):
        columns = expand(source[:2], row_count, plane_taps(1))
        return jax.nn.relu(
            jnp.einsum("ok,kzn->ozn", primal_in, columns, preferred_element_type=jnp.float32)
        ).astype(jnp.bfloat16)

    def first_skip_branch(source):
        return jnp.zeros((hidden_count, row_count, cell_count), jnp.bfloat16)

    return lax.switch(
        net_mode, [first_dual_branch, first_primal_branch, first_skip_branch], extended
    )


def second_layer(hidden, row_count, net_mode, weights):
    dual_in, dual_out, primal_in, primal_out = weights
    dual_count = dual_in.shape[0]
    cell_count = hidden.shape[2]

    def second_dual_branch(source):
        return collapse(source[:dual_count], dual_out, row_count, plane_taps(0))

    def second_primal_branch(source):
        return collapse(source, primal_out, row_count, plane_taps(1))

    def second_skip_branch(source):
        return jnp.zeros((row_count, cell_count), jnp.float32)

    return lax.switch(
        net_mode, [second_dual_branch, second_primal_branch, second_skip_branch], hidden
    )


def network_update(channels, net_mode, weights):
    row_count = channels.shape[1]
    extended = padded_2(channels, (("gz", 1),), 1)
    hidden = first_layer(extended, row_count, net_mode, weights)
    hidden = padded_2(as_sent(hidden), (("gz", 1),), 1).astype(hidden.dtype)
    return second_layer(hidden, row_count, net_mode, weights)


def band_local(padded, shifts, projector, band_mode, row_count):
    cell_count = padded.shape[1]
    groups = shifts.shape[0]
    group_width = cell_count // groups

    def forward(source):
        starts = row_count - 1 + shifts
        windows = jax.vmap(
            lambda start_row: lax.dynamic_slice_in_dim(source, start_row, row_count + 2, 0)
        )(starts)
        by_group = jnp.zeros((row_count, groups, group_width), jnp.float32)
        for tap_row in range(3):
            window_rows = lax.slice_in_dim(windows, tap_row, tap_row + row_count, axis=1)
            by_group = by_group + jnp.einsum(
                "gzp,pgc->zgc",
                window_rows,
                projector[tap_row].reshape(cell_count, groups, group_width),
                preferred_element_type=jnp.float32,
            )
        return by_group.reshape(row_count, cell_count)

    def adjoint(source):
        starts = row_count - 1 - shifts
        grouped = source.reshape(source.shape[0], groups, group_width)
        windows = jax.vmap(
            lambda column, start_row: lax.dynamic_slice_in_dim(column, start_row, row_count + 2, 0),
            in_axes=(1, 0),
        )(grouped, starts)
        summed = jnp.zeros((row_count, cell_count), jnp.float32)
        for tap_row in range(3):
            window_rows = lax.slice_in_dim(windows, 2 - tap_row, 2 - tap_row + row_count, axis=1)
            summed = summed + jnp.einsum(
                "gzc,pgc->zp",
                window_rows,
                projector[tap_row].reshape(cell_count, groups, group_width),
                preferred_element_type=jnp.float32,
            )
        return summed

    def band_skip_branch(source):
        return jnp.zeros((row_count, cell_count), jnp.float32)

    return lax.switch(band_mode, [forward, adjoint, band_skip_branch], padded)


def band_apply(values, shifts, projector, band_mode):
    row_count = values.shape[0]
    rounded = values.astype(jnp.bfloat16)
    padded = padded_2(rounded, (("gz", 0),), row_count)
    return band_local(padded, shifts, projector, band_mode, row_count)


def per_device(
    start_volume, sinogram, offsets, projector, dual_in, dual_out, primal_in, primal_out
):
    slab_count = start_volume.shape[0]
    row_count = start_volume.shape[1]
    cell_count = start_volume.shape[2]
    segment_count = lax.axis_size("segment")
    segment_index = lax.axis_index("segment")
    weights = (dual_in, dual_out, primal_in, primal_out)
    tick_count = ITERS * segment_count + slab_count - 1
    empty_rows = jnp.zeros((row_count, cell_count), jnp.float32)
    band_mode = jnp.where(segment_index == 0, 0, jnp.where(segment_index == 2, 1, 2)).astype(
        jnp.int32
    )
    net_mode = jnp.where(segment_index == 1, 0, jnp.where(segment_index == 3, 1, 2)).astype(
        jnp.int32
    )
    is_primal = segment_index == 3

    def plan(tick_number):
        behind = tick_number - segment_index
        member = jnp.mod(behind, segment_count)
        rounds = (behind - member) // segment_count
        active = (behind >= 0) & (rounds < ITERS)
        return (member, rounds, active)

    def net_channels(dual_state, volume_now, message, member):
        dual_stack = jnp.stack([dual_state, message, sinogram[member]])
        primal_stack = jnp.stack([volume_now, message, empty_rows])
        return jnp.where(is_primal, primal_stack, dual_stack).astype(jnp.bfloat16)

    def advance(tick_number, carried):
        message, volumes, duals = carried
        member, rounds, active = plan(tick_number)
        current = jnp.where(rounds == 0, start_volume[member], message)
        band_input = jnp.where(segment_index == 0, current, message)
        band_out = band_apply(band_input, offsets[member], projector, band_mode)
        channels = net_channels(duals[member], volumes[member], message, member)
        net_out = network_update(channels, net_mode, weights)
        dual_next = duals[member] + net_out
        volume_next = volumes[member] + net_out
        duals = jnp.where(active & (segment_index == 1), duals.at[member].set(dual_next), duals)
        volumes = jnp.where(active & is_primal, volumes.at[member].set(volume_next), volumes)
        outgoing = jnp.where(
            segment_index == 1, dual_next, jnp.where(is_primal, volume_next, band_out)
        )
        return (shifted_2(as_sent(outgoing), "segment", 1).astype(outgoing.dtype), volumes, duals)

    initial = (empty_rows, start_volume, jnp.zeros_like(start_volume))
    outcome = lax.fori_loop(0, tick_count, advance, initial)
    finished = outcome[1]
    kept = jnp.where(segment_index == segment_count - 1, finished, jnp.zeros_like(finished))
    return lax.psum_scatter(kept, "segment", scatter_dimension=0, tiled=True)


def solution(mesh):
    in_specs = (P(None, "gz", None), P(None, "gz", None), P(), P(), P(), P(), P(), P())
    out_specs = P("segment", "gz", None)
    return jax.shard_map(
        per_device, mesh=mesh, in_specs=in_specs, out_specs=out_specs, check_vma=False
    )
```

profile of v0, /device:TPU:29, one launch (start us, length us, event | category | flops | bytes accessed | tf_op | source)
XLA Modules:
  0.0 537.2 jit_solution(3383540230341129382)
XLA Ops:
  9.1 8.7 %copy.96 = bf16[3,1024,1024]{1,2,0:T(8,128)(2,1)} copy(bf16[3,1024,1024]{2,1,0:T(8,128)(2,1)} %param.26) | data formatting | bytes 12582912
  18.6 489.6 %while.24 = (s32[]{:T(128)}, bf16[16,1024]{1,0:T(8,128)(2,1)S(1)}, f32[4,16,1024]{2,1,0:T(8,128)S(1)}, f32[4,16,1024]{2,1,0:T(8,128)}, pred[]{:T(512)}, /*index=...) while((s32[]{:T(128)}, bf16[16,1024]{1,0:T(8,128)(2,1)S(1)}, ...), condition=%wide.region_11.12_spmd.clone, body=%wide.region_0.11_spmd.clone.sunk | while | flops 287464576 | bytes 52902068 | solution.py:253
  43.2 6.2 %conditional.9 = (bf16[16,1024]{1,0:T(8,128)(2,1)S(1)}) conditional(s32[]{:T(128)} %get-tuple-element.1084, (s32[4,8]{1,0:T(4,128)}, s32[]{:T(128)}, bf16[48,1024]{1,0:T(8,128)(2,1)S(1)}, bf16[3,1024,1024]{1,2,0:T(8,128)(2,1)}) %tuple.239, (bf16[48,1024]{1,0:T(8,128)(2,1)S(1)}, s32[4,8]{1,0:T(4,128)}, s32[]{:T(128)}, ...), branch_computations={%region_7.7_spmd, %region_8.8_spmd, %region_9.9_spmd} | conditional | flops 100712520 | bytes 20119880 | solution.py:194
  50.1 11.0 %collective-permute-start.6 = (bf16[16,1024]{1,0:T(8,128)(2,1)S(1)}, bf16[16,1024]{1,0:T(8,128)(2,1)S(1)}, u32[]{:S(2)}, u32[]{:S(2)}) collective-permute-start(bf16[16,1024]{1,0:T(8,128)(2,1)S(1)} %select_convert_fusion.2), channel_id=1, source_target_pairs={{0,64},{64,128},{128,192},{192,0},{1,65},{65,129},{129,193},{193,1... | collective-permute-start | bytes 98312 | tf_op jit(solution)/shard_map/while/body/eval_jaxpr/ppermute | solution.py:35
  64.3 7.5 %collective-permute-start.2 = (bf16[3,1,1024]{2,1,0:T(2,128)(2,1)S(1)}, bf16[3,1,1024]{2,1,0:T(2,128)(2,1)S(1)}, u32[]{:S(2)}, u32[]{:S(2)}) collective-permute-start(bf16[3,1,1024]{2,1,0:T(2,128)(2,1)S(1)} %get-tuple-element.986), channel_id=1, source_target_pairs={{1,0},{2,1},{3,2},{4,3},{5,4},{6,5},{7,6},{8,7},{9,8},{10,9},{11,1... | collective-permute-start | bytes 18440 | tf_op jit(solution)/shard_map/while/body/eval_jaxpr/ppermute | solution.py:21
  93.9 12.1 %collective-permute-start.6 = (bf16[16,1024]{1,0:T(8,128)(2,1)S(1)}, bf16[16,1024]{1,0:T(8,128)(2,1)S(1)}, u32[]{:S(2)}, u32[]{:S(2)}) collective-permute-start(bf16[16,1024]{1,0:T(8,128)(2,1)S(1)} %select_convert_fusion.2), channel_id=1, source_target_pairs={{0,64},{64,128},{128,192},{192,0},{1,65},{65,129},{129,193},{193,1... | collective-permute-start | bytes 98312 | tf_op jit(solution)/shard_map/while/body/eval_jaxpr/ppermute | solution.py:35
  109.2 7.0 %collective-permute-start.2 = (bf16[3,1,1024]{2,1,0:T(2,128)(2,1)S(1)}, bf16[3,1,1024]{2,1,0:T(2,128)(2,1)S(1)}, u32[]{:S(2)}, u32[]{:S(2)}) collective-permute-start(bf16[3,1,1024]{2,1,0:T(2,128)(2,1)S(1)} %get-tuple-element.986), channel_id=1, source_target_pairs={{1,0},{2,1},{3,2},{4,3},{5,4},{6,5},{7,6},{8,7},{9,8},{10,9},{11,1... | collective-permute-start | bytes 18440 | tf_op jit(solution)/shard_map/while/body/eval_jaxpr/ppermute | solution.py:21
  131.3 6.2 %conditional.9 = (bf16[16,1024]{1,0:T(8,128)(2,1)S(1)}) conditional(s32[]{:T(128)} %get-tuple-element.1084, (s32[4,8]{1,0:T(4,128)}, s32[]{:T(128)}, bf16[48,1024]{1,0:T(8,128)(2,1)S(1)}, bf16[3,1024,1024]{1,2,0:T(8,128)(2,1)}) %tuple.239, (bf16[48,1024]{1,0:T(8,128)(2,1)S(1)}, s32[4,8]{1,0:T(4,128)}, s32[]{:T(128)}, ...), branch_computations={%region_7.7_spmd, %region_8.8_spmd, %region_9.9_spmd} | conditional | flops 100712520 | bytes 20119880 | solution.py:194
  138.3 12.1 %collective-permute-start.6 = (bf16[16,1024]{1,0:T(8,128)(2,1)S(1)}, bf16[16,1024]{1,0:T(8,128)(2,1)S(1)}, u32[]{:S(2)}, u32[]{:S(2)}) collective-permute-start(bf16[16,1024]{1,0:T(8,128)(2,1)S(1)} %select_convert_fusion.2), channel_id=1, source_target_pairs={{0,64},{64,128},{128,192},{192,0},{1,65},{65,129},{129,193},{193,1... | collective-permute-start | bytes 98312 | tf_op jit(solution)/shard_map/while/body/eval_jaxpr/ppermute | solution.py:35
  153.6 7.0 %collective-permute-start.2 = (bf16[3,1,1024]{2,1,0:T(2,128)(2,1)S(1)}, bf16[3,1,1024]{2,1,0:T(2,128)(2,1)S(1)}, u32[]{:S(2)}, u32[]{:S(2)}) collective-permute-start(bf16[3,1,1024]{2,1,0:T(2,128)(2,1)S(1)} %get-tuple-element.986), channel_id=1, source_target_pairs={{1,0},{2,1},{3,2},{4,3},{5,4},{6,5},{7,6},{8,7},{9,8},{10,9},{11,1... | collective-permute-start | bytes 18440 | tf_op jit(solution)/shard_map/while/body/eval_jaxpr/ppermute | solution.py:21
  175.8 6.2 %conditional.9 = (bf16[16,1024]{1,0:T(8,128)(2,1)S(1)}) conditional(s32[]{:T(128)} %get-tuple-element.1084, (s32[4,8]{1,0:T(4,128)}, s32[]{:T(128)}, bf16[48,1024]{1,0:T(8,128)(2,1)S(1)}, bf16[3,1024,1024]{1,2,0:T(8,128)(2,1)}) %tuple.239, (bf16[48,1024]{1,0:T(8,128)(2,1)S(1)}, s32[4,8]{1,0:T(4,128)}, s32[]{:T(128)}, ...), branch_computations={%region_7.7_spmd, %region_8.8_spmd, %region_9.9_spmd} | conditional | flops 100712520 | bytes 20119880 | solution.py:194
  182.7 12.1 %collective-permute-start.6 = (bf16[16,1024]{1,0:T(8,128)(2,1)S(1)}, bf16[16,1024]{1,0:T(8,128)(2,1)S(1)}, u32[]{:S(2)}, u32[]{:S(2)}) collective-permute-start(bf16[16,1024]{1,0:T(8,128)(2,1)S(1)} %select_convert_fusion.2), channel_id=1, source_target_pairs={{0,64},{64,128},{128,192},{192,0},{1,65},{65,129},{129,193},{193,1... | collective-permute-start | bytes 98312 | tf_op jit(solution)/shard_map/while/body/eval_jaxpr/ppermute | solution.py:35
  198.0 7.0 %collective-permute-start.2 = (bf16[3,1,1024]{2,1,0:T(2,128)(2,1)S(1)}, bf16[3,1,1024]{2,1,0:T(2,128)(2,1)S(1)}, u32[]{:S(2)}, u32[]{:S(2)}) collective-permute-start(bf16[3,1,1024]{2,1,0:T(2,128)(2,1)S(1)} %get-tuple-element.986), channel_id=1, source_target_pairs={{1,0},{2,1},{3,2},{4,3},{5,4},{6,5},{7,6},{8,7},{9,8},{10,9},{11,1... | collective-permute-start | bytes 18440 | tf_op jit(solution)/shard_map/while/body/eval_jaxpr/ppermute | solution.py:21
  227.1 12.1 %collective-permute-start.6 = (bf16[16,1024]{1,0:T(8,128)(2,1)S(1)}, bf16[16,1024]{1,0:T(8,128)(2,1)S(1)}, u32[]{:S(2)}, u32[]{:S(2)}) collective-permute-start(bf16[16,1024]{1,0:T(8,128)(2,1)S(1)} %select_convert_fusion.2), channel_id=1, source_target_pairs={{0,64},{64,128},{128,192},{192,0},{1,65},{65,129},{129,193},{193,1... | collective-permute-start | bytes 98312 | tf_op jit(solution)/shard_map/while/body/eval_jaxpr/ppermute | solution.py:35
  242.4 7.0 %collective-permute-start.2 = (bf16[3,1,1024]{2,1,0:T(2,128)(2,1)S(1)}, bf16[3,1,1024]{2,1,0:T(2,128)(2,1)S(1)}, u32[]{:S(2)}, u32[]{:S(2)}) collective-permute-start(bf16[3,1,1024]{2,1,0:T(2,128)(2,1)S(1)} %get-tuple-element.986), channel_id=1, source_target_pairs={{1,0},{2,1},{3,2},{4,3},{5,4},{6,5},{7,6},{8,7},{9,8},{10,9},{11,1... | collective-permute-start | bytes 18440 | tf_op jit(solution)/shard_map/while/body/eval_jaxpr/ppermute | solution.py:21
  264.6 6.2 %conditional.9 = (bf16[16,1024]{1,0:T(8,128)(2,1)S(1)}) conditional(s32[]{:T(128)} %get-tuple-element.1084, (s32[4,8]{1,0:T(4,128)}, s32[]{:T(128)}, bf16[48,1024]{1,0:T(8,128)(2,1)S(1)}, bf16[3,1024,1024]{1,2,0:T(8,128)(2,1)}) %tuple.239, (bf16[48,1024]{1,0:T(8,128)(2,1)S(1)}, s32[4,8]{1,0:T(4,128)}, s32[]{:T(128)}, ...), branch_computations={%region_7.7_spmd, %region_8.8_spmd, %region_9.9_spmd} | conditional | flops 100712520 | bytes 20119880 | solution.py:194
  271.5 12.1 %collective-permute-start.6 = (bf16[16,1024]{1,0:T(8,128)(2,1)S(1)}, bf16[16,1024]{1,0:T(8,128)(2,1)S(1)}, u32[]{:S(2)}, u32[]{:S(2)}) collective-permute-start(bf16[16,1024]{1,0:T(8,128)(2,1)S(1)} %select_convert_fusion.2), channel_id=1, source_target_pairs={{0,64},{64,128},{128,192},{192,0},{1,65},{65,129},{129,193},{193,1... | collective-permute-start | bytes 98312 | tf_op jit(solution)/shard_map/while/body/eval_jaxpr/ppermute | solution.py:35
  286.8 7.0 %collective-permute-start.2 = (bf16[3,1,1024]{2,1,0:T(2,128)(2,1)S(1)}, bf16[3,1,1024]{2,1,0:T(2,128)(2,1)S(1)}, u32[]{:S(2)}, u32[]{:S(2)}) collective-permute-start(bf16[3,1,1024]{2,1,0:T(2,128)(2,1)S(1)} %get-tuple-element.986), channel_id=1, source_target_pairs={{1,0},{2,1},{3,2},{4,3},{5,4},{6,5},{7,6},{8,7},{9,8},{10,9},{11,1... | collective-permute-start | bytes 18440 | tf_op jit(solution)/shard_map/while/body/eval_jaxpr/ppermute | solution.py:21
  309.0 6.2 %conditional.9 = (bf16[16,1024]{1,0:T(8,128)(2,1)S(1)}) conditional(s32[]{:T(128)} %get-tuple-element.1084, (s32[4,8]{1,0:T(4,128)}, s32[]{:T(128)}, bf16[48,1024]{1,0:T(8,128)(2,1)S(1)}, bf16[3,1024,1024]{1,2,0:T(8,128)(2,1)}) %tuple.239, (bf16[48,1024]{1,0:T(8,128)(2,1)S(1)}, s32[4,8]{1,0:T(4,128)}, s32[]{:T(128)}, ...), branch_computations={%region_7.7_spmd, %region_8.8_spmd, %region_9.9_spmd} | conditional | flops 100712520 | bytes 20119880 | solution.py:194
  315.9 12.1 %collective-permute-start.6 = (bf16[16,1024]{1,0:T(8,128)(2,1)S(1)}, bf16[16,1024]{1,0:T(8,128)(2,1)S(1)}, u32[]{:S(2)}, u32[]{:S(2)}) collective-permute-start(bf16[16,1024]{1,0:T(8,128)(2,1)S(1)} %select_convert_fusion.2), channel_id=1, source_target_pairs={{0,64},{64,128},{128,192},{192,0},{1,65},{65,129},{129,193},{193,1... | collective-permute-start | bytes 98312 | tf_op jit(solution)/shard_map/while/body/eval_jaxpr/ppermute | solution.py:35
  331.2 7.1 %collective-permute-start.2 = (bf16[3,1,1024]{2,1,0:T(2,128)(2,1)S(1)}, bf16[3,1,1024]{2,1,0:T(2,128)(2,1)S(1)}, u32[]{:S(2)}, u32[]{:S(2)}) collective-permute-start(bf16[3,1,1024]{2,1,0:T(2,128)(2,1)S(1)} %get-tuple-element.986), channel_id=1, source_target_pairs={{1,0},{2,1},{3,2},{4,3},{5,4},{6,5},{7,6},{8,7},{9,8},{10,9},{11,1... | collective-permute-start | bytes 18440 | tf_op jit(solution)/shard_map/while/body/eval_jaxpr/ppermute | solution.py:21
  353.5 6.2 %conditional.9 = (bf16[16,1024]{1,0:T(8,128)(2,1)S(1)}) conditional(s32[]{:T(128)} %get-tuple-element.1084, (s32[4,8]{1,0:T(4,128)}, s32[]{:T(128)}, bf16[48,1024]{1,0:T(8,128)(2,1)S(1)}, bf16[3,1024,1024]{1,2,0:T(8,128)(2,1)}) %tuple.239, (bf16[48,1024]{1,0:T(8,128)(2,1)S(1)}, s32[4,8]{1,0:T(4,128)}, s32[]{:T(128)}, ...), branch_computations={%region_7.7_spmd, %region_8.8_spmd, %region_9.9_spmd} | conditional | flops 100712520 | bytes 20119880 | solution.py:194
  360.4 12.1 %collective-permute-start.6 = (bf16[16,1024]{1,0:T(8,128)(2,1)S(1)}, bf16[16,1024]{1,0:T(8,128)(2,1)S(1)}, u32[]{:S(2)}, u32[]{:S(2)}) collective-permute-start(bf16[16,1024]{1,0:T(8,128)(2,1)S(1)} %select_convert_fusion.2), channel_id=1, source_target_pairs={{0,64},{64,128},{128,192},{192,0},{1,65},{65,129},{129,193},{193,1... | collective-permute-start | bytes 98312 | tf_op jit(solution)/shard_map/while/body/eval_jaxpr/ppermute | solution.py:35
  375.7 7.4 %collective-permute-start.2 = (bf16[3,1,1024]{2,1,0:T(2,128)(2,1)S(1)}, bf16[3,1,1024]{2,1,0:T(2,128)(2,1)S(1)}, u32[]{:S(2)}, u32[]{:S(2)}) collective-permute-start(bf16[3,1,1024]{2,1,0:T(2,128)(2,1)S(1)} %get-tuple-element.986), channel_id=1, source_target_pairs={{1,0},{2,1},{3,2},{4,3},{5,4},{6,5},{7,6},{8,7},{9,8},{10,9},{11,1... | collective-permute-start | bytes 18440 | tf_op jit(solution)/shard_map/while/body/eval_jaxpr/ppermute | solution.py:21
  398.3 6.2 %conditional.9 = (bf16[16,1024]{1,0:T(8,128)(2,1)S(1)}) conditional(s32[]{:T(128)} %get-tuple-element.1084, (s32[4,8]{1,0:T(4,128)}, s32[]{:T(128)}, bf16[48,1024]{1,0:T(8,128)(2,1)S(1)}, bf16[3,1024,1024]{1,2,0:T(8,128)(2,1)}) %tuple.239, (bf16[48,1024]{1,0:T(8,128)(2,1)S(1)}, s32[4,8]{1,0:T(4,128)}, s32[]{:T(128)}, ...), branch_computations={%region_7.7_spmd, %region_8.8_spmd, %region_9.9_spmd} | conditional | flops 100712520 | bytes 20119880 | solution.py:194
  405.2 12.1 %collective-permute-start.6 = (bf16[16,1024]{1,0:T(8,128)(2,1)S(1)}, bf16[16,1024]{1,0:T(8,128)(2,1)S(1)}, u32[]{:S(2)}, u32[]{:S(2)}) collective-permute-start(bf16[16,1024]{1,0:T(8,128)(2,1)S(1)} %select_convert_fusion.2), channel_id=1, source_target_pairs={{0,64},{64,128},{128,192},{192,0},{1,65},{65,129},{129,193},{193,1... | collective-permute-start | bytes 98312 | tf_op jit(solution)/shard_map/while/body/eval_jaxpr/ppermute | solution.py:35
  420.5 7.4 %collective-permute-start.2 = (bf16[3,1,1024]{2,1,0:T(2,128)(2,1)S(1)}, bf16[3,1,1024]{2,1,0:T(2,128)(2,1)S(1)}, u32[]{:S(2)}, u32[]{:S(2)}) collective-permute-start(bf16[3,1,1024]{2,1,0:T(2,128)(2,1)S(1)} %get-tuple-element.986), channel_id=1, source_target_pairs={{1,0},{2,1},{3,2},{4,3},{5,4},{6,5},{7,6},{8,7},{9,8},{10,9},{11,1... | collective-permute-start | bytes 18440 | tf_op jit(solution)/shard_map/while/body/eval_jaxpr/ppermute | solution.py:21
  443.1 6.2 %conditional.9 = (bf16[16,1024]{1,0:T(8,128)(2,1)S(1)}) conditional(s32[]{:T(128)} %get-tuple-element.1084, (s32[4,8]{1,0:T(4,128)}, s32[]{:T(128)}, bf16[48,1024]{1,0:T(8,128)(2,1)S(1)}, bf16[3,1024,1024]{1,2,0:T(8,128)(2,1)}) %tuple.239, (bf16[48,1024]{1,0:T(8,128)(2,1)S(1)}, s32[4,8]{1,0:T(4,128)}, s32[]{:T(128)}, ...), branch_computations={%region_7.7_spmd, %region_8.8_spmd, %region_9.9_spmd} | conditional | flops 100712520 | bytes 20119880 | solution.py:194
  450.0 12.1 %collective-permute-start.6 = (bf16[16,1024]{1,0:T(8,128)(2,1)S(1)}, bf16[16,1024]{1,0:T(8,128)(2,1)S(1)}, u32[]{:S(2)}, u32[]{:S(2)}) collective-permute-start(bf16[16,1024]{1,0:T(8,128)(2,1)S(1)} %select_convert_fusion.2), channel_id=1, source_target_pairs={{0,64},{64,128},{128,192},{192,0},{1,65},{65,129},{129,193},{193,1... | collective-permute-start | bytes 98312 | tf_op jit(solution)/shard_map/while/body/eval_jaxpr/ppermute | solution.py:35
  465.3 7.4 %collective-permute-start.2 = (bf16[3,1,1024]{2,1,0:T(2,128)(2,1)S(1)}, bf16[3,1,1024]{2,1,0:T(2,128)(2,1)S(1)}, u32[]{:S(2)}, u32[]{:S(2)}) collective-permute-start(bf16[3,1,1024]{2,1,0:T(2,128)(2,1)S(1)} %get-tuple-element.986), channel_id=1, source_target_pairs={{1,0},{2,1},{3,2},{4,3},{5,4},{6,5},{7,6},{8,7},{9,8},{10,9},{11,1... | collective-permute-start | bytes 18440 | tf_op jit(solution)/shard_map/while/body/eval_jaxpr/ppermute | solution.py:21
  494.8 12.1 %collective-permute-start.6 = (bf16[16,1024]{1,0:T(8,128)(2,1)S(1)}, bf16[16,1024]{1,0:T(8,128)(2,1)S(1)}, u32[]{:S(2)}, u32[]{:S(2)}) collective-permute-start(bf16[16,1024]{1,0:T(8,128)(2,1)S(1)} %select_convert_fusion.2), channel_id=1, source_target_pairs={{0,64},{64,128},{128,192},{192,0},{1,65},{65,129},{129,193},{193,1... | collective-permute-start | bytes 98312 | tf_op jit(solution)/shard_map/while/body/eval_jaxpr/ppermute | solution.py:35
  508.9 21.4 %reduce-scatter.2.cloned.1.call-done = f32[1,16,1024]{2,1,0:T(8,128)} async-done(((f32[4,16,1024]{2,1,0:T(8,128)}), f32[1,16,1024]{2,1,0:T(8,128)}) %reduce-scatter.2.cloned.1.call-update) | async-done | bytes 65552 | tf_op jit(solution)/shard_map/reduce_scatter | solution.py:256
  (513 shorter events, 307.8 us)
Async XLA Ops:
  6.5 523.8 %reduce-scatter.2.cloned.1.call-start = ((), (), s32[]{:S(2)}) async-start(), calls=%async_computation.1 | async-start | bytes 327680 | tf_op jit(solution)/shard_map/reduce_scatter | solution.py:256
  20.5 13.8 %collective-permute-start.2 = (bf16[3,1,1024]{2,1,0:T(2,128)(2,1)S(1)}, bf16[3,1,1024]{2,1,0:T(2,128)(2,1)S(1)}, u32[]{:S(2)}, u32[]{:S(2)}) collective-permute-start(bf16[3,1,1024]{2,1,0:T(2,128)(2,1)S(1)} %get-tuple-element.986), channel_id=1, source_target_pairs={{1,0},{2,1},{3,2},{4,3},{5,4},{6,5},{7,6},{8,7},{9,8},{10,9},{11,1... | collective-permute-start | bytes 18440 | tf_op jit(solution)/shard_map/while/body/eval_jaxpr/ppermute | solution.py:21
  26.5 16.7 %collective-permute-start.1 = (bf16[16,1024]{1,0:T(8,128)(2,1)S(1)}, bf16[16,1024]{1,0:T(8,128)(2,1)S(1)}, u32[]{:S(2)}, u32[]{:S(2)}) collective-permute-start(bf16[16,1024]{1,0:T(8,128)(2,1)S(1)} %get-tuple-element.982), channel_id=1, source_target_pairs={{0,1},{1,2},{2,3},{3,4},{4,5},{5,6},{6,7},{7,8},{8,9},{9,10},{10,1... | collective-permute-start | bytes 98312 | tf_op jit(solution)/shard_map/while/body/eval_jaxpr/ppermute | solution.py:19
  28.9 14.2 %collective-permute-start = (bf16[16,1024]{1,0:T(8,128)(2,1)S(1)}, bf16[16,1024]{1,0:T(8,128)(2,1)S(1)}, u32[]{:S(2)}, u32[]{:S(2)}) collective-permute-start(bf16[16,1024]{1,0:T(8,128)(2,1)S(1)} %get-tuple-element.982), channel_id=1, source_target_pairs={{1,0},{2,1},{3,2},{4,3},{5,4},{6,5},{7,6},{8,7},{9,8},{10,9},{11,1... | collective-permute-start | bytes 98312 | tf_op jit(solution)/shard_map/while/body/eval_jaxpr/ppermute | solution.py:21
  34.7 14.7 %collective-permute-start.4 = (bf16[64,1,1024]{2,0,1:T(8,128)(2,1)S(1)}, bf16[64,1,1024]{2,0,1:T(8,128)(2,1)S(1)}, u32[]{:S(2)}, u32[]{:S(2)}) collective-permute-start(bf16[64,1,1024]{2,0,1:T(8,128)(2,1)S(1)} %get-tuple-element.988), channel_id=1, source_target_pairs={{1,0},{2,1},{3,2},{4,3},{5,4},{6,5},{7,6},{8,7},{9,8},{10,9},{11,1... | collective-permute-start | bytes 393224 | tf_op jit(solution)/shard_map/while/body/eval_jaxpr/ppermute | solution.py:21
  64.3 13.8 %collective-permute-start.2 = (bf16[3,1,1024]{2,1,0:T(2,128)(2,1)S(1)}, bf16[3,1,1024]{2,1,0:T(2,128)(2,1)S(1)}, u32[]{:S(2)}, u32[]{:S(2)}) collective-permute-start(bf16[3,1,1024]{2,1,0:T(2,128)(2,1)S(1)} %get-tuple-element.986), channel_id=1, source_target_pairs={{1,0},{2,1},{3,2},{4,3},{5,4},{6,5},{7,6},{8,7},{9,8},{10,9},{11,1... | collective-permute-start | bytes 18440 | tf_op jit(solution)/shard_map/while/body/eval_jaxpr/ppermute | solution.py:21
  78.5 14.7 %collective-permute-start.4 = (bf16[64,1,1024]{2,0,1:T(8,128)(2,1)S(1)}, bf16[64,1,1024]{2,0,1:T(8,128)(2,1)S(1)}, u32[]{:S(2)}, u32[]{:S(2)}) collective-permute-start(bf16[64,1,1024]{2,0,1:T(8,128)(2,1)S(1)} %get-tuple-element.988), channel_id=1, source_target_pairs={{1,0},{2,1},{3,2},{4,3},{5,4},{6,5},{7,6},{8,7},{9,8},{10,9},{11,1... | collective-permute-start | bytes 393224 | tf_op jit(solution)/shard_map/while/body/eval_jaxpr/ppermute | solution.py:21
  93.9 13.4 %collective-permute-start.6 = (bf16[16,1024]{1,0:T(8,128)(2,1)S(1)}, bf16[16,1024]{1,0:T(8,128)(2,1)S(1)}, u32[]{:S(2)}, u32[]{:S(2)}) collective-permute-start(bf16[16,1024]{1,0:T(8,128)(2,1)S(1)} %select_convert_fusion.2), channel_id=1, source_target_pairs={{0,64},{64,128},{128,192},{192,0},{1,65},{65,129},{129,193},{193,1... | collective-permute-start | bytes 98312 | tf_op jit(solution)/shard_map/while/body/eval_jaxpr/ppermute | solution.py:35
  109.2 13.3 %collective-permute-start.2 = (bf16[3,1,1024]{2,1,0:T(2,128)(2,1)S(1)}, bf16[3,1,1024]{2,1,0:T(2,128)(2,1)S(1)}, u32[]{:S(2)}, u32[]{:S(2)}) collective-permute-start(bf16[3,1,1024]{2,1,0:T(2,128)(2,1)S(1)} %get-tuple-element.986), channel_id=1, source_target_pairs={{1,0},{2,1},{3,2},{4,3},{5,4},{6,5},{7,6},{8,7},{9,8},{10,9},{11,1... | collective-permute-start | bytes 18440 | tf_op jit(solution)/shard_map/while/body/eval_jaxpr/ppermute | solution.py:21
  122.9 14.7 %collective-permute-start.4 = (bf16[64,1,1024]{2,0,1:T(8,128)(2,1)S(1)}, bf16[64,1,1024]{2,0,1:T(8,128)(2,1)S(1)}, u32[]{:S(2)}, u32[]{:S(2)}) collective-permute-start(bf16[64,1,1024]{2,0,1:T(8,128)(2,1)S(1)} %get-tuple-element.988), channel_id=1, source_target_pairs={{1,0},{2,1},{3,2},{4,3},{5,4},{6,5},{7,6},{8,7},{9,8},{10,9},{11,1... | collective-permute-start | bytes 393224 | tf_op jit(solution)/shard_map/while/body/eval_jaxpr/ppermute | solution.py:21
  138.3 13.4 %collective-permute-start.6 = (bf16[16,1024]{1,0:T(8,128)(2,1)S(1)}, bf16[16,1024]{1,0:T(8,128)(2,1)S(1)}, u32[]{:S(2)}, u32[]{:S(2)}) collective-permute-start(bf16[16,1024]{1,0:T(8,128)(2,1)S(1)} %select_convert_fusion.2), channel_id=1, source_target_pairs={{0,64},{64,128},{128,192},{192,0},{1,65},{65,129},{129,193},{193,1... | collective-permute-start | bytes 98312 | tf_op jit(solution)/shard_map/while/body/eval_jaxpr/ppermute | solution.py:35
  167.3 14.7 %collective-permute-start.4 = (bf16[64,1,1024]{2,0,1:T(8,128)(2,1)S(1)}, bf16[64,1,1024]{2,0,1:T(8,128)(2,1)S(1)}, u32[]{:S(2)}, u32[]{:S(2)}) collective-permute-start(bf16[64,1,1024]{2,0,1:T(8,128)(2,1)S(1)} %get-tuple-element.988), channel_id=1, source_target_pairs={{1,0},{2,1},{3,2},{4,3},{5,4},{6,5},{7,6},{8,7},{9,8},{10,9},{11,1... | collective-permute-start | bytes 393224 | tf_op jit(solution)/shard_map/while/body/eval_jaxpr/ppermute | solution.py:21
  182.7 13.4 %collective-permute-start.6 = (bf16[16,1024]{1,0:T(8,128)(2,1)S(1)}, bf16[16,1024]{1,0:T(8,128)(2,1)S(1)}, u32[]{:S(2)}, u32[]{:S(2)}) collective-permute-start(bf16[16,1024]{1,0:T(8,128)(2,1)S(1)} %select_convert_fusion.2), channel_id=1, source_target_pairs={{0,64},{64,128},{128,192},{192,0},{1,65},{65,129},{129,193},{193,1... | collective-permute-start | bytes 98312 | tf_op jit(solution)/shard_map/while/body/eval_jaxpr/ppermute | solution.py:35
  211.7 14.7 %collective-permute-start.4 = (bf16[64,1,1024]{2,0,1:T(8,128)(2,1)S(1)}, bf16[64,1,1024]{2,0,1:T(8,128)(2,1)S(1)}, u32[]{:S(2)}, u32[]{:S(2)}) collective-permute-start(bf16[64,1,1024]{2,0,1:T(8,128)(2,1)S(1)} %get-tuple-element.988), channel_id=1, source_target_pairs={{1,0},{2,1},{3,2},{4,3},{5,4},{6,5},{7,6},{8,7},{9,8},{10,9},{11,1... | collective-permute-start | bytes 393224 | tf_op jit(solution)/shard_map/while/body/eval_jaxpr/ppermute | solution.py:21
  227.1 13.4 %collective-permute-start.6 = (bf16[16,1024]{1,0:T(8,128)(2,1)S(1)}, bf16[16,1024]{1,0:T(8,128)(2,1)S(1)}, u32[]{:S(2)}, u32[]{:S(2)}) collective-permute-start(bf16[16,1024]{1,0:T(8,128)(2,1)S(1)} %select_convert_fusion.2), channel_id=1, source_target_pairs={{0,64},{64,128},{128,192},{192,0},{1,65},{65,129},{129,193},{193,1... | collective-permute-start | bytes 98312 | tf_op jit(solution)/shard_map/while/body/eval_jaxpr/ppermute | solution.py:35
  256.1 14.7 %collective-permute-start.4 = (bf16[64,1,1024]{2,0,1:T(8,128)(2,1)S(1)}, bf16[64,1,1024]{2,0,1:T(8,128)(2,1)S(1)}, u32[]{:S(2)}, u32[]{:S(2)}) collective-permute-start(bf16[64,1,1024]{2,0,1:T(8,128)(2,1)S(1)} %get-tuple-element.988), channel_id=1, source_target_pairs={{1,0},{2,1},{3,2},{4,3},{5,4},{6,5},{7,6},{8,7},{9,8},{10,9},{11,1... | collective-permute-start | bytes 393224 | tf_op jit(solution)/shard_map/while/body/eval_jaxpr/ppermute | solution.py:21
  271.5 13.4 %collective-permute-start.6 = (bf16[16,1024]{1,0:T(8,128)(2,1)S(1)}, bf16[16,1024]{1,0:T(8,128)(2,1)S(1)}, u32[]{:S(2)}, u32[]{:S(2)}) collective-permute-start(bf16[16,1024]{1,0:T(8,128)(2,1)S(1)} %select_convert_fusion.2), channel_id=1, source_target_pairs={{0,64},{64,128},{128,192},{192,0},{1,65},{65,129},{129,193},{193,1... | collective-permute-start | bytes 98312 | tf_op jit(solution)/shard_map/while/body/eval_jaxpr/ppermute | solution.py:35
  286.8 13.3 %collective-permute-start.2 = (bf16[3,1,1024]{2,1,0:T(2,128)(2,1)S(1)}, bf16[3,1,1024]{2,1,0:T(2,128)(2,1)S(1)}, u32[]{:S(2)}, u32[]{:S(2)}) collective-permute-start(bf16[3,1,1024]{2,1,0:T(2,128)(2,1)S(1)} %get-tuple-element.986), channel_id=1, source_target_pairs={{1,0},{2,1},{3,2},{4,3},{5,4},{6,5},{7,6},{8,7},{9,8},{10,9},{11,1... | collective-permute-start | bytes 18440 | tf_op jit(solution)/shard_map/while/body/eval_jaxpr/ppermute | solution.py:21
  300.5 14.7 %collective-permute-start.4 = (bf16[64,1,1024]{2,0,1:T(8,128)(2,1)S(1)}, bf16[64,1,1024]{2,0,1:T(8,128)(2,1)S(1)}, u32[]{:S(2)}, u32[]{:S(2)}) collective-permute-start(bf16[64,1,1024]{2,0,1:T(8,128)(2,1)S(1)} %get-tuple-element.988), channel_id=1, source_target_pairs={{1,0},{2,1},{3,2},{4,3},{5,4},{6,5},{7,6},{8,7},{9,8},{10,9},{11,1... | collective-permute-start | bytes 393224 | tf_op jit(solution)/shard_map/while/body/eval_jaxpr/ppermute | solution.py:21
  315.9 13.4 %collective-permute-start.6 = (bf16[16,1024]{1,0:T(8,128)(2,1)S(1)}, bf16[16,1024]{1,0:T(8,128)(2,1)S(1)}, u32[]{:S(2)}, u32[]{:S(2)}) collective-permute-start(bf16[16,1024]{1,0:T(8,128)(2,1)S(1)} %select_convert_fusion.2), channel_id=1, source_target_pairs={{0,64},{64,128},{128,192},{192,0},{1,65},{65,129},{129,193},{193,1... | collective-permute-start | bytes 98312 | tf_op jit(solution)/shard_map/while/body/eval_jaxpr/ppermute | solution.py:35
  331.2 13.4 %collective-permute-start.2 = (bf16[3,1,1024]{2,1,0:T(2,128)(2,1)S(1)}, bf16[3,1,1024]{2,1,0:T(2,128)(2,1)S(1)}, u32[]{:S(2)}, u32[]{:S(2)}) collective-permute-start(bf16[3,1,1024]{2,1,0:T(2,128)(2,1)S(1)} %get-tuple-element.986), channel_id=1, source_target_pairs={{1,0},{2,1},{3,2},{4,3},{5,4},{6,5},{7,6},{8,7},{9,8},{10,9},{11,1... | collective-permute-start | bytes 18440 | tf_op jit(solution)/shard_map/while/body/eval_jaxpr/ppermute | solution.py:21
  345.1 14.7 %collective-permute-start.4 = (bf16[64,1,1024]{2,0,1:T(8,128)(2,1)S(1)}, bf16[64,1,1024]{2,0,1:T(8,128)(2,1)S(1)}, u32[]{:S(2)}, u32[]{:S(2)}) collective-permute-start(bf16[64,1,1024]{2,0,1:T(8,128)(2,1)S(1)} %get-tuple-element.988), channel_id=1, source_target_pairs={{1,0},{2,1},{3,2},{4,3},{5,4},{6,5},{7,6},{8,7},{9,8},{10,9},{11,1... | collective-permute-start | bytes 393224 | tf_op jit(solution)/shard_map/while/body/eval_jaxpr/ppermute | solution.py:21
  360.4 13.4 %collective-permute-start.6 = (bf16[16,1024]{1,0:T(8,128)(2,1)S(1)}, bf16[16,1024]{1,0:T(8,128)(2,1)S(1)}, u32[]{:S(2)}, u32[]{:S(2)}) collective-permute-start(bf16[16,1024]{1,0:T(8,128)(2,1)S(1)} %select_convert_fusion.2), channel_id=1, source_target_pairs={{0,64},{64,128},{128,192},{192,0},{1,65},{65,129},{129,193},{193,1... | collective-permute-start | bytes 98312 | tf_op jit(solution)/shard_map/while/body/eval_jaxpr/ppermute | solution.py:35
  375.7 13.7 %collective-permute-start.2 = (bf16[3,1,1024]{2,1,0:T(2,128)(2,1)S(1)}, bf16[3,1,1024]{2,1,0:T(2,128)(2,1)S(1)}, u32[]{:S(2)}, u32[]{:S(2)}) collective-permute-start(bf16[3,1,1024]{2,1,0:T(2,128)(2,1)S(1)} %get-tuple-element.986), channel_id=1, source_target_pairs={{1,0},{2,1},{3,2},{4,3},{5,4},{6,5},{7,6},{8,7},{9,8},{10,9},{11,1... | collective-permute-start | bytes 18440 | tf_op jit(solution)/shard_map/while/body/eval_jaxpr/ppermute | solution.py:21
  389.8 14.7 %collective-permute-start.4 = (bf16[64,1,1024]{2,0,1:T(8,128)(2,1)S(1)}, bf16[64,1,1024]{2,0,1:T(8,128)(2,1)S(1)}, u32[]{:S(2)}, u32[]{:S(2)}) collective-permute-start(bf16[64,1,1024]{2,0,1:T(8,128)(2,1)S(1)} %get-tuple-element.988), channel_id=1, source_target_pairs={{1,0},{2,1},{3,2},{4,3},{5,4},{6,5},{7,6},{8,7},{9,8},{10,9},{11,1... | collective-permute-start | bytes 393224 | tf_op jit(solution)/shard_map/while/body/eval_jaxpr/ppermute | solution.py:21
  405.2 13.4 %collective-permute-start.6 = (bf16[16,1024]{1,0:T(8,128)(2,1)S(1)}, bf16[16,1024]{1,0:T(8,128)(2,1)S(1)}, u32[]{:S(2)}, u32[]{:S(2)}) collective-permute-start(bf16[16,1024]{1,0:T(8,128)(2,1)S(1)} %select_convert_fusion.2), channel_id=1, source_target_pairs={{0,64},{64,128},{128,192},{192,0},{1,65},{65,129},{129,193},{193,1... | collective-permute-start | bytes 98312 | tf_op jit(solution)/shard_map/while/body/eval_jaxpr/ppermute | solution.py:35
  420.5 13.7 %collective-permute-start.2 = (bf16[3,1,1024]{2,1,0:T(2,128)(2,1)S(1)}, bf16[3,1,1024]{2,1,0:T(2,128)(2,1)S(1)}, u32[]{:S(2)}, u32[]{:S(2)}) collective-permute-start(bf16[3,1,1024]{2,1,0:T(2,128)(2,1)S(1)} %get-tuple-element.986), channel_id=1, source_target_pairs={{1,0},{2,1},{3,2},{4,3},{5,4},{6,5},{7,6},{8,7},{9,8},{10,9},{11,1... | collective-permute-start | bytes 18440 | tf_op jit(solution)/shard_map/while/body/eval_jaxpr/ppermute | solution.py:21
  434.6 14.7 %collective-permute-start.4 = (bf16[64,1,1024]{2,0,1:T(8,128)(2,1)S(1)}, bf16[64,1,1024]{2,0,1:T(8,128)(2,1)S(1)}, u32[]{:S(2)}, u32[]{:S(2)}) collective-permute-start(bf16[64,1,1024]{2,0,1:T(8,128)(2,1)S(1)} %get-tuple-element.988), channel_id=1, source_target_pairs={{1,0},{2,1},{3,2},{4,3},{5,4},{6,5},{7,6},{8,7},{9,8},{10,9},{11,1... | collective-permute-start | bytes 393224 | tf_op jit(solution)/shard_map/while/body/eval_jaxpr/ppermute | solution.py:21
  450.0 13.4 %collective-permute-start.6 = (bf16[16,1024]{1,0:T(8,128)(2,1)S(1)}, bf16[16,1024]{1,0:T(8,128)(2,1)S(1)}, u32[]{:S(2)}, u32[]{:S(2)}) collective-permute-start(bf16[16,1024]{1,0:T(8,128)(2,1)S(1)} %select_convert_fusion.2), channel_id=1, source_target_pairs={{0,64},{64,128},{128,192},{192,0},{1,65},{65,129},{129,193},{193,1... | collective-permute-start | bytes 98312 | tf_op jit(solution)/shard_map/while/body/eval_jaxpr/ppermute | solution.py:35
  465.3 13.7 %collective-permute-start.2 = (bf16[3,1,1024]{2,1,0:T(2,128)(2,1)S(1)}, bf16[3,1,1024]{2,1,0:T(2,128)(2,1)S(1)}, u32[]{:S(2)}, u32[]{:S(2)}) collective-permute-start(bf16[3,1,1024]{2,1,0:T(2,128)(2,1)S(1)} %get-tuple-element.986), channel_id=1, source_target_pairs={{1,0},{2,1},{3,2},{4,3},{5,4},{6,5},{7,6},{8,7},{9,8},{10,9},{11,1... | collective-permute-start | bytes 18440 | tf_op jit(solution)/shard_map/while/body/eval_jaxpr/ppermute | solution.py:21
  479.4 14.7 %collective-permute-start.4 = (bf16[64,1,1024]{2,0,1:T(8,128)(2,1)S(1)}, bf16[64,1,1024]{2,0,1:T(8,128)(2,1)S(1)}, u32[]{:S(2)}, u32[]{:S(2)}) collective-permute-start(bf16[64,1,1024]{2,0,1:T(8,128)(2,1)S(1)} %get-tuple-element.988), channel_id=1, source_target_pairs={{1,0},{2,1},{3,2},{4,3},{5,4},{6,5},{7,6},{8,7},{9,8},{10,9},{11,1... | collective-permute-start | bytes 393224 | tf_op jit(solution)/shard_map/while/body/eval_jaxpr/ppermute | solution.py:21
  494.8 13.4 %collective-permute-start.6 = (bf16[16,1024]{1,0:T(8,128)(2,1)S(1)}, bf16[16,1024]{1,0:T(8,128)(2,1)S(1)}, u32[]{:S(2)}, u32[]{:S(2)}) collective-permute-start(bf16[16,1024]{1,0:T(8,128)(2,1)S(1)} %select_convert_fusion.2), channel_id=1, source_target_pairs={{0,64},{64,128},{128,192},{192,0},{1,65},{65,129},{129,193},{193,1... | collective-permute-start | bytes 98312 | tf_op jit(solution)/shard_map/while/body/eval_jaxpr/ppermute | solution.py:35
  (93 other events, 968.4 us)
Sparse Core Ops, SparseCore 0:
  509.1 21.2 reduce-scatter.1
where the time goes:
time: 546 us; the launch traced here: 537 us
  starting transfers between devices  365 us (67%)
  local copies, waits for them, and re-layouts  75.3 us (14%)
  other arithmetic  45.7 us (8%)
  waiting for transfers between devices  21.6 us (4%)
  between operations  13.4 us (2%)
  matrix products  12.8 us (2%)
    ppermute x33, starting transfers between devices, padded_2(): lax.ppermute(head, axis, [((i + 1) % count, i) for i in range(ends)])  167 us
    ppermute x11, starting transfers between devices, shifted_2(): return lax.ppermute(value, axis, pairs)  132 us
    ppermute x33, starting transfers between devices, padded_2(): lax.ppermute(tail, axis, [(i, (i + 1) % count) for i in range(ends)])  65.4 us
    slice x11, local copies, waits for them, and re-layouts, adjoint(): projector[tap_row].reshape(cell_count, groups, group_width)  39.3 us
    reduce_scatter x1, waiting for transfers between devices, per_device(): return lax.psum_scatter(kept, 'segment', scatter_dimension=0, tiled=True)  21.4 us
    select_n x11, other arithmetic, advance(): jnp.where(active & (segment_index == 1), duals.at[member].set(dual_next),...  13.7 us
    dot_general x33, matrix products, adjoint(): jnp.einsum('gzc,pgc->zp', window_rows, projector[tap_row].reshape(cell_co...  12.8 us
  transfers between devices with their start and end apart: 78, of which 1 were waited for; matrix products, arithmetic and copies ran while one was open for 17% of the time, Pallas kernels for 0%

commit v1 on v0

v1 whole, which is shorter than its diff:
```python
import functools

import jax
import jax.numpy as jnp
from jax import lax
from jax.experimental import pallas as pl
from jax.experimental.pallas import tpu as pltpu
from jax.sharding import PartitionSpec as P

IMG = 32
NCOL = 128
ITERS = 2
BF = jnp.bfloat16
F32 = jnp.float32
MESH = pl.DeviceIdType.MESH

BASE = 24
GROUPS = 3
STEP = 6


def iota(shape, dim):
    return lax.broadcasted_iota(jnp.int32, shape, dim)


def one_hot(mask):
    return jnp.where(mask, 1.0, 0.0).astype(BF)


def dot(a, b):
    return jnp.dot(a, b, preferred_element_type=F32)


def dual_keep(step, width):
    col = iota((1, width), 1) % NCOL + step
    return (col >= 0) & (col < NCOL)


def primal_keep(down, across, width):
    lane = iota((1, width), 1)
    row = lane // IMG + down
    col = lane % IMG + across
    return (row >= 0) & (row < IMG) & (col >= 0) & (col < IMG)


def shifted(x, offset, keep):
    if offset == 0:
        return x
    width = x.shape[-1]
    return jnp.where(keep, pltpu.roll(x, (-offset) % width, 1), 0.0)


def first_weights(w, taps, rows_in_k, out_ref):
    for z in range(STEP):
        q = iota((3 * taps, rows_in_k), 0)
        c = iota((3 * taps, rows_in_k), 1)
        zz = c % 8
        j = c // 8
        sel = one_hot((q == (zz - z) * taps + j) & (j < taps))
        count = w.shape[0]
        out_ref[z * count : (z + 1) * count, :] = dot(w, sel).astype(BF)


def second_weights(w, taps, row_count, first_row, total_rows, out_ref):
    count = w.shape[1]
    pack = 128 // count
    q = iota((pack * 3 * taps, 3 * taps), 0)
    t = iota((pack * 3 * taps, 3 * taps), 1)
    stacked = dot(one_hot(q % (3 * taps) == t), w).astype(BF)
    spread = one_hot(iota((count, 128), 0) == iota((count, 128), 1) % count)
    wide = dot(stacked, spread)
    qq = iota(wide.shape, 0) // (3 * taps)
    lane = iota(wide.shape, 1) // count
    wide = jnp.where(qq == lane, wide, 0.0).astype(BF)
    height = taps * row_count
    hidden_rows = row_count + 2
    for m in range(-(-hidden_rows // pack)):
        r = iota((height, pack * 3 * taps), 0)
        c = iota((height, pack * 3 * taps), 1)
        y = m * pack + c // (3 * taps)
        row = first_row + y - 1
        mask = (c % (3 * taps)) == (y - r % row_count) * taps + r // row_count
        mask = mask & (y < hidden_rows) & (row >= 0) & (row < total_rows)
        out_ref[:, m * 128 : (m + 1) * 128] = dot(one_hot(mask), wide).astype(BF)


def kernel(
    sizes,
    sv_hbm,
    sino_hbm,
    off_ref,
    proj_hbm,
    din_hbm,
    dout_hbm,
    pin_hbm,
    pout_hbm,
    out_ref,
    field,
    sino,
    dual,
    proj,
    din,
    dout,
    pin,
    pout,
    ext,
    far_s,
    far_r,
    sino_s,
    sino_r,
    far_f,
    g,
    u,
    xf,
    xs,
    xa,
    wd,
    vd,
    wp,
    vp,
    cold,
    colp,
    hid,
    res,
    load_sem,
    send_sem,
    recv_sem,
    sino_ssem,
    sino_rsem,
):
    seg_count, gz_count, rows, cells = sizes
    views = cells // NCOL
    total = gz_count * rows
    seg = lax.axis_index("segment")
    me = lax.axis_index("gz")
    right = lax.rem(me + 1, gz_count)
    left = lax.rem(me + gz_count - 1, gz_count)
    right2 = lax.rem(me + 2, gz_count)
    left2 = lax.rem(me + gz_count - 2, gz_count)
    first_row = me * rows

    barrier = pltpu.get_barrier_semaphore()
    for other in (left, right, left2, right2):
        pl.semaphore_signal(barrier, inc=1, device_id={"gz": other}, device_id_type=MESH)

    loads = [
        pltpu.make_async_copy(src, dst, load_sem.at[i])
        for i, (src, dst) in enumerate(
            [
                (sv_hbm.at[seg], field),
                (sino_hbm.at[seg], sino),
                (din_hbm, din),
                (dout_hbm, dout),
                (pin_hbm, pin),
                (pout_hbm, pout),
                (proj_hbm, proj),
            ]
        )
    ]
    for copy in loads:
        copy.start()

    def remote(src, dst, ssem, rsem, other):
        return pltpu.make_async_remote_copy(
            src_ref=src,
            dst_ref=dst,
            send_sem=ssem,
            recv_sem=rsem,
            device_id={"gz": other},
            device_id_type=MESH,
        )

    def copies(e):
        own = ext.at[e, pl.ds(16, 16)]
        return [
            remote(own, ext.at[e, pl.ds(0, 16)], send_sem.at[e, 0], recv_sem.at[e, 0], right),
            remote(own, ext.at[e, pl.ds(32, 16)], send_sem.at[e, 1], recv_sem.at[e, 1], left),
            remote(far_s.at[e, 1], far_r.at[e, 0], send_sem.at[e, 2], recv_sem.at[e, 2], right2),
            remote(far_s.at[e, 0], far_r.at[e, 1], send_sem.at[e, 3], recv_sem.at[e, 3], left2),
        ]

    def send(e, ref):
        ext[e, 16:32, :] = ref[...].astype(BF)
        far_s[e, 0] = ref[0:2, :].astype(BF)
        far_s[e, 1] = ref[rows - 2 : rows, :].astype(BF)
        for copy in copies(e):
            copy.start()

    def receive(e):
        for copy in copies(e):
            copy.wait()

        @pl.when(me == 0)
        def _():
            ext[e, 0:16, :] = jnp.zeros((16, cells), BF)

        @pl.when(me == gz_count - 1)
        def _():
            ext[e, 32:48, :] = jnp.zeros((16, cells), BF)

        @pl.when(me <= 1)
        def _():
            far_r[e, 0] = jnp.zeros((2, cells), BF)

        @pl.when(me >= gz_count - 2)
        def _():
            far_r[e, 1] = jnp.zeros((2, cells), BF)

    sino_copies = [
        remote(sino_s.at[1], sino_r.at[0], sino_ssem.at[0], sino_rsem.at[0], right),
        remote(sino_s.at[0], sino_r.at[1], sino_ssem.at[1], sino_rsem.at[1], left),
    ]

    loads[0].wait()
    loads[1].wait()
    sino_s[0] = sino[0:2, :].astype(BF)
    sino_s[1] = sino[rows - 2 : rows, :].astype(BF)
    pl.semaphore_wait(barrier, 4)
    send(0, field)
    for copy in sino_copies:
        copy.start()

    u[...] = jnp.zeros(u.shape, F32)
    far_f[...] = jnp.zeros(far_f.shape, F32)
    for k in range(3):
        g[k, :, 0:8, :] = jnp.zeros((views, 8, NCOL), F32)
        g[k, :, 56:64, :] = jnp.zeros((views, 8, NCOL), F32)
    hid[576:640, :] = jnp.zeros((64, hid.shape[1]), BF)
    dual[...] = jnp.zeros(dual.shape, F32)
    for i in range(2, 6):
        loads[i].wait()
    first_weights(din[...], 9, wd.shape[1], wd)
    first_weights(pin[...], 18, wp.shape[1], wp)
    second_weights(dout[...], 3, rows, first_row, total, vd)
    second_weights(pout[...], 9, rows, first_row, total, vp)

    for copy in sino_copies:
        copy.wait()
    xs[2 : 2 + rows, :] = sino[...]
    xs[0:2, :] = jnp.where(me == 0, 0.0, sino_r[0].astype(F32))
    xs[rows + 2 : rows + 4, :] = jnp.where(me == gz_count - 1, 0.0, sino_r[1].astype(F32))
    loads[6].wait()

    row = iota((24, 1), 0)
    inside = (row < rows + 4) & (first_row + row >= 2) & (first_row + row - 2 < total)

    def network(x_reads, steps, keeps, per_step, w_ref, col, v_ref, out_count):
        pad = w_ref.shape[1] - len(steps) * per_step
        for t in range(GROUPS):
            stack = jnp.concatenate([read(t * STEP) for read in x_reads], 0)
            pieces = [shifted(stack, offset, keep) for offset, keep in zip(steps, keeps)]
            if pad:
                pieces.append(jnp.zeros((pad, cells), F32))
            col[t] = jnp.concatenate(pieces, 0).astype(BF)
        height = w_ref.shape[0]
        depth = v_ref.shape[1]
        out_rows = v_ref.shape[0]
        for n in range(cells // 256):
            lanes = slice(n * 256, (n + 1) * 256)
            for t in range(GROUPS):
                value = dot(w_ref[...], col[t, :, lanes])
                hid[t * height : (t + 1) * height, :] = jnp.maximum(value, 0.0).astype(BF)
            res[0:out_rows, lanes] = dot(v_ref[...], hid[0:depth, :])
        total_value = None
        for s, (offset, keep) in enumerate(zip(steps, keeps)):
            part = shifted(res[s * rows : (s + 1) * rows, :], offset, keep)
            total_value = part if total_value is None else total_value + part
        return total_value

    def rows_of(ref):
        return lambda start: ref[start : start + 8, :]

    def read_u(start):
        low = BASE - 2 + start
        return jnp.concatenate([u[w, low : low + 8, :] for w in range(views)], 1)

    dual_steps = [-1, 0, 1]
    dual_keeps = [dual_keep(s, cells) for s in dual_steps]
    primal_pairs = [(dy, dx) for dy in (-1, 0, 1) for dx in (-1, 0, 1)]
    primal_steps = [dy * IMG + dx for dy, dx in primal_pairs]
    primal_keeps = [primal_keep(dy, dx, cells) for dy, dx in primal_pairs]

    def iteration(it, carry):
        ef = 2 * it
        eh = 2 * it + 1
        receive(ef)
        far_f[0:2, :] = far_r[ef, 0].astype(F32)
        far_f[2:4, :] = far_r[ef, 1].astype(F32)
        ext[ef, 48:64, :] = far_f[...].astype(BF)
        for k in range(3):
            product = dot(ext[ef], proj[k])
            for w in range(views):
                lanes = slice(w * NCOL, (w + 1) * NCOL)
                g[k, w, 8:56, :] = product[0:48, lanes]
                g[k, w, 6:8, :] = product[48:50, lanes]
                g[k, w, 56:58, :] = product[50:52, lanes]
        for w in range(views):
            lanes = slice(w * NCOL, (w + 1) * NCOL)
            shift = off_ref[seg, w]
            value = g[0, w, pl.ds(BASE - 3 + shift, 24), :]
            value = value + g[1, w, pl.ds(BASE - 2 + shift, 24), :]
            value = value + g[2, w, pl.ds(BASE - 1 + shift, 24), :]
            xa[:, lanes] = jnp.where(inside, value, 0.0)
        xf[0:2, :] = ext[ef, 0:16, :].astype(F32)[14:16, :]
        xf[2 : 2 + rows, :] = ext[ef, 16:32, :].astype(F32)
        xf[rows + 2 : rows + 4, :] = ext[ef, 32:48, :].astype(F32)[0:2, :]
        dual[...] += network(
            [read_u, rows_of(xa), rows_of(xs)], dual_steps, dual_keeps, 24, wd, cold, vd, 3
        )
        send(eh, dual)
        receive(eh)
        for w in range(views):
            lanes = slice(w * NCOL, (w + 1) * NCOL)
            u[w, 8:56, :] = ext[eh, 0:48, lanes].astype(F32)
            u[w, 6:8, :] = far_r[eh, 0, :, lanes].astype(F32)
            u[w, 56:58, :] = far_r[eh, 1, :, lanes].astype(F32)
        back = None
        for k in range(3):
            window = jnp.concatenate(
                [
                    u[w, pl.ds(BASE - 1 - k - off_ref[seg, w], 24), :]
                    for w in range(views)
                ],
                1,
            ).astype(BF)
            part = lax.dot_general(
                window, proj[k], (((1,), (1,)), ((), ())), preferred_element_type=F32
            )
            back = part if back is None else back + part
        xa[...] = jnp.where(inside, back, 0.0)
        field[...] += network(
            [rows_of(xf), rows_of(xa)], primal_steps, primal_keeps, 16, wp, colp, vp, 9
        )

        @pl.when(it < ITERS - 1)
        def _():
            send(ef + 2, field)

        return carry

    lax.fori_loop(0, ITERS, iteration, 0)
    out_ref[0] = field[...]


def per_device(
    start_volume, sinogram, offsets, projector, dual_in, dual_out, primal_in, primal_out
):
    _, rows, cells = start_volume.shape
    seg_count = lax.axis_size("segment")
    gz_count = lax.axis_size("gz")
    sizes = (seg_count, gz_count, rows, cells)
    exchanges = 2 * ITERS
    any_spec = pl.BlockSpec(memory_space=pl.ANY)
    vm = pltpu.VMEM
    return pl.pallas_call(
        functools.partial(kernel, sizes),
        out_shape=jax.ShapeDtypeStruct((1, rows, cells), F32),
        in_specs=[any_spec, any_spec, pl.BlockSpec(memory_space=pltpu.SMEM)] + [any_spec] * 5,
        out_specs=pl.BlockSpec(memory_space=pltpu.VMEM),
        scratch_shapes=[
            vm((rows, cells), F32),
            vm((rows, cells), F32),
            vm((rows, cells), F32),
            vm(projector.shape, BF),
            vm(dual_in.shape, BF),
            vm(dual_out.shape, BF),
            vm(primal_in.shape, BF),
            vm(primal_out.shape, BF),
            vm((exchanges, 64, cells), BF),
            vm((exchanges, 2, 2, cells), BF),
            vm((exchanges, 2, 2, cells), BF),
            vm((2, 2, cells), BF),
            vm((2, 2, cells), BF),
            vm((16, cells), F32),
            vm((3, cells // NCOL, 64, NCOL), F32),
            vm((cells // NCOL, 64, NCOL), F32),
            vm((24, cells), F32),
            vm((24, cells), F32),
            vm((24, cells), F32),
            vm((6 * 32, 80), BF),
            vm((3 * rows, 640), BF),
            vm((6 * 64, 144), BF),
            vm((9 * rows, 1152), BF),
            vm((GROUPS, 80, cells), BF),
            vm((GROUPS, 144, cells), BF),
            vm((1152, 256), BF),
            vm((9 * rows, cells), F32),
            pltpu.SemaphoreType.DMA((7,)),
            pltpu.SemaphoreType.DMA((exchanges, 4)),
            pltpu.SemaphoreType.DMA((exchanges, 4)),
            pltpu.SemaphoreType.DMA((2,)),
            pltpu.SemaphoreType.DMA((2,)),
        ],
        compiler_params=pltpu.CompilerParams(
            collective_id=0, has_side_effects=True, vmem_limit_bytes=60 * 1024 * 1024
        ),
        name="reconstruct",
    )(start_volume, sinogram, offsets, projector, dual_in, dual_out, primal_in, primal_out)


def solution(mesh):
    in_specs = (P(None, "gz", None), P(None, "gz", None), P(), P(), P(), P(), P(), P())
    out_specs = P("segment", "gz", None)
    return jax.shard_map(
        per_device, mesh=mesh, in_specs=in_specs, out_specs=out_specs, check_vma=False
    )
```

time: 546 us -> 43.1 us (0.08)
  the two profiles are of different devices: /device:TPU:29 before, /device:TPU:1 now
where the time goes in v1:
time: 43.1 us; the launch traced here: 43 us
  Pallas kernels  40.1 us (93%)
  local copies, waits for them, and re-layouts  2.88 us (7%)
    pallas_call x1, Pallas kernels, per_device(): pl.pallas_call(functools.partial(kernel, sizes), out_shape=jax.ShapeDtype...  40.1 us
    unnamed x2, local copies, waits for them, and re-layouts  2.88 us

profile of v1, /device:TPU:1, one launch (start us, length us, event | category | flops | bytes accessed | tf_op | source)
XLA Modules:
  0.0 43.0 jit_solution(16482584093605198543)
XLA Ops:
  0.0 1.4 %copy.9.pin_hbm = bf16[64,54]{1,0:T(8,128)(2,1)} copy(bf16[64,54]{0,1:T(8,128)(2,1)} %param.14) | data formatting | bytes 13824 | tf_op args[6]
  1.4 40.1 %reconstruct.1 = f32[1,16,1024]{2,1,0:T(8,128)} custom-call(f32[4,16,1024]{2,1,0:T(8,128)} %sv_hbm.1, f32[4,16,1024]{2,1,0:T(8,128)} %sino_hbm.1, s32[4,8]{1,0:T(4,128)} %off_ref.1, bf16[3,1024,1024]{2,1,0:T(8,128)(2,1)} %proj_hbm.1, bf16[32,27]{1,0:T(8,128)(2,1)} %din_hbm.1, bf16[9,32]{1,0:T(8,128)(2,1)} %dout_hbm.1, bf16[64,54]{1,0:T(8,128)(2,1)} %copy.9.pin_hbm, ...), custom_call_target="tpu_custom_call" | custom-call | tf_op jit(solution)/shard_map/reconstruct/pallas_call | solution.py:355
  41.5 1.5 %copy.11 = f32[1,16,1024]{2,1,0:T(8,128)} copy(f32[1,16,1024]{2,1,0:T(8,128)} %reconstruct.1) | data formatting | bytes 131072
